TPU v7x, 256 devices: a whole 4x4x8 slice. The times are simulated.
256 devices in a mesh: seq: 64 (over z, x, core), tp: 4 (over y).
Axes of the slice: x: 4, y: 4, z: 8, core: 2. Of those that a mesh axis runs over, the one named last changes fastest.
Arguments:
- tokens: bfloat16 [8192, 2048], P('seq'), may hold values from -6 to 6
- input_heads: bfloat16 [8192, 4096], P('seq', 'tp'), may hold values from -6 to 6
- z_gate: bfloat16 [8192, 4096], P('seq', 'tp'), may hold values from -6 to 6
- b_proj: bfloat16 [8192, 128], P('seq'), may hold values from -0.5 to 0.5
- c_proj: bfloat16 [8192, 128], P('seq'), may hold values from -0.5 to 0.5
- step_size: float32 [8192, 64], P('seq', 'tp'), may hold values from 0.5 to 2
- decay_log: float32 [8192, 64], P('seq', 'tp'), as said below
- skip_gain: float32 [64], P('tp'), may hold values from 0.5 to 2
- init_state: float32 [64, 64, 128], P('tp'), may hold values from -48 to 48
- norm_gain: float32 [4096], P('tp'), may hold values from 0.1 to 1.9
- out_weight: bfloat16 [4096, 2048], P('tp'), may hold values from -0.09375 to 0.09375
- moe_gain: float32 [2048], replicated, may hold values from 0.1 to 1.9
- routes: int32 [8192, 2], P('seq'), may hold values from 0 to 63, all different within a row; in each aligned block of 128 rows (0 to 127, 128 to 255, ...) at most 8 rows name the same one
- route_weights: float32 [8192, 2], P('seq'), may hold values from 0.2 to 1
- w_gate: bfloat16 [64, 2048, 2048], P('seq', None, 'tp'), may hold values from -0.125 to 0.125
- w_up: bfloat16 [64, 2048, 2048], P('seq', None, 'tp'), may hold values from -0.125 to 0.125
- w_down: bfloat16 [64, 2048, 2048], P('seq', 'tp'), may hold values from -0.125 to 0.125
Outputs:
- mixed_out: bfloat16 [8192, 2048], P('seq', 'tp')
Inputs may be any that keep to these rules, and one draw needn't show every extreme that they name: `decay_log`: every entry is negative. `routes`: the two experts of a row differ. In each aligned block of 128 rows (the rows of one device) no expert is named by more than 8 rows, a bound that some block reaches.
All inputs are finite; a program needn't handle non-finite values.
Results may differ from a plain program's by a relative error of at most 0.02.
Values may be sent and summed in bfloat16 or wider, within the bound.
A program may use at most 128 MiB of HBM per device.

v0:
```python
import jax
import jax.numpy as jnp
from jax import lax
from jax.sharding import PartitionSpec as P


def entering(part, axis, combine, identity):
    place = lax.axis_index(axis)
    gathered = jax.tree.map(lambda a: lax.all_gather(a, axis), part)
    state = jax.tree.map(lambda a, e: jnp.zeros_like(a) + jnp.asarray(e, a.dtype), part, identity)

    def one(turn, state):
        return combine(
            state, jax.tree.map(lambda a: lax.dynamic_index_in_dim(a, turn, 0, False), gathered)
        )

    return lax.fori_loop(0, place, one, state)


def rms_rows(values, scale_gain):
    wide_vals = values.astype(jnp.float32)
    mean_sq = jnp.mean(wide_vals * wide_vals, axis=-1, keepdims=True)
    return (wide_vals * lax.rsqrt(mean_sq + 1e-05) * scale_gain).astype(jnp.bfloat16)


def merge_carry(first_part, second_part):
    decay_first, state_first = first_part
    decay_second, state_second = second_part
    return (decay_first * decay_second, decay_second[:, None, None] * state_first + state_second)


def body(
    tokens,
    input_heads,
    z_gate,
    b_proj,
    c_proj,
    step_size,
    decay_log,
    skip_gain,
    init_state,
    norm_gain,
    out_weight,
    moe_gain,
    routes,
    route_weights,
    w_gate,
    w_up,
    w_down,
):
    highest = lax.Precision.HIGHEST
    tok_rows = input_heads.shape[0]
    head_count = step_size.shape[1]
    head_size = init_state.shape[1]
    x_wide = input_heads.astype(jnp.float32).reshape(tok_rows, head_count, head_size)
    input_matrix_broad = b_proj.astype(jnp.float32)
    c_wide = c_proj.astype(jnp.float32)
    cum_decay = jnp.cumsum(decay_log, axis=0)
    end_decay = cum_decay[-1]
    positions = jnp.arange(tok_rows, dtype=jnp.int32)
    causal = positions[:, None] >= positions[None, :]
    scores = jnp.einsum("in,jn->ij", c_proj, b_proj, preferred_element_type=jnp.float32)
    cum_heads = cum_decay.T
    log_gap = cum_heads[:, :, None] - cum_heads[:, None, :]
    decay_mat = jnp.where(causal, jnp.exp(jnp.where(causal, log_gap, 0.0)), 0.0)
    mix_weights = decay_mat * scores[None] * step_size.T[:, None, :]
    intra_part = jnp.einsum("hij,jhp->ihp", mix_weights, x_wide, precision=highest)
    weighted = (jnp.exp(end_decay[None, :] - cum_decay) * step_size)[:, :, None] * x_wide
    local_state = jnp.einsum("jhp,jn->hpn", weighted, input_matrix_broad, precision=highest)
    block_decay = jnp.exp(end_decay)
    prior_decay, prior_state = entering(
        (block_decay, local_state),
        "seq",
        merge_carry,
        (jnp.ones_like(block_decay), jnp.zeros_like(local_state)),
    )
    arriving_rows = prior_decay[:, None, None] * init_state + prior_state
    inter_part = (
        jnp.einsum("in,hpn->ihp", c_wide, arriving_rows, precision=highest)
        * jnp.exp(cum_decay)[:, :, None]
    )
    ssd_out = intra_part + inter_part + skip_gain[None, :, None] * x_wide
    z_wide = z_gate.astype(jnp.float32).reshape(tok_rows, head_count, head_size)
    gated_vals = ssd_out * jax.nn.silu(z_wide)
    gated_vals = gated_vals * lax.rsqrt(
        jnp.mean(gated_vals * gated_vals, axis=2, keepdims=True) + 1e-05
    )
    normed = (gated_vals.reshape(tok_rows, head_count * head_size) * norm_gain).astype(jnp.bfloat16)
    partial_value = jnp.dot(normed, out_weight, preferred_element_type=jnp.float32)
    model_width = out_weight.shape[1]
    width_share = model_width // lax.axis_size("tp")
    col_start = lax.axis_index("tp") * width_share
    seq_count = lax.axis_size("seq")
    expert_count = w_gate.shape[0] * seq_count
    slot_count = 4 * tok_rows // seq_count
    top_count = routes.shape[1]
    flat_expert = routes.reshape(-1)
    onehot = (flat_expert[:, None] == jnp.arange(expert_count, dtype=jnp.int32)[None, :]).astype(
        jnp.int32
    )
    earlier_count = jnp.cumsum(onehot, axis=0) - onehot
    slot_rank = jnp.sum(earlier_count * onehot, axis=1)
    placed = flat_expert * slot_count + slot_rank
    owners = jnp.arange(top_count * tok_rows, dtype=jnp.int32) // top_count
    source = jnp.full((expert_count * slot_count,), tok_rows, jnp.int32).at[placed].set(owners)
    proj_sum = lax.psum(partial_value.astype(jnp.bfloat16), "tp").astype(jnp.float32)
    hidden_full = (tokens.astype(jnp.float32) + proj_sum).astype(jnp.bfloat16)
    moe_in = rms_rows(hidden_full, moe_gain)
    outgoing = jnp.take(moe_in, source, axis=0, mode="fill", fill_value=0).reshape(
        expert_count, slot_count, model_width
    )
    hidden = lax.dynamic_slice_in_dim(hidden_full, col_start, width_share, 1)
    moe_rows = lax.all_to_all(outgoing, "seq", split_axis=0, concat_axis=0, tiled=True)
    src_count, item_count, full_width = moe_rows.shape
    flat_rows = moe_rows.reshape(src_count * item_count, full_width)
    gate_val = jnp.dot(flat_rows, w_gate[0], preferred_element_type=jnp.float32)
    up_val = jnp.dot(flat_rows, w_up[0], preferred_element_type=jnp.float32)
    act_vals = (jax.nn.silu(gate_val) * up_val).astype(jnp.bfloat16)
    down_val = jnp.dot(act_vals, w_down[0], preferred_element_type=jnp.float32)
    summed = lax.psum_scatter(down_val.astype(jnp.bfloat16), "tp", scatter_dimension=1, tiled=True)
    results = summed.reshape(src_count, item_count, -1)
    returned = lax.all_to_all(results, "seq", split_axis=0, concat_axis=0, tiled=True)
    chosen_indices = jnp.take(
        returned.reshape(expert_count * slot_count, width_share), placed, axis=0
    ).reshape(tok_rows, top_count, width_share)
    mixed_out = hidden.astype(jnp.float32) + jnp.sum(
        route_weights[:, :, None] * chosen_indices.astype(jnp.float32), axis=1
    )
    return mixed_out.astype(jnp.bfloat16)


def solution(mesh):
    in_specs = (
        P("seq", None),
        P("seq", "tp"),
        P("seq", "tp"),
        P("seq", None),
        P("seq", None),
        P("seq", "tp"),
        P("seq", "tp"),
        P("tp"),
        P("tp", None, None),
        P("tp"),
        P("tp", None),
        P(),
        P("seq", None),
        P("seq", None),
        P("seq", None, "tp"),
        P("seq", None, "tp"),
        P("seq", "tp", None),
    )
    out_specs = P("seq", "tp")
    return jax.shard_map(body, mesh=mesh, in_specs=in_specs, out_specs=out_specs, check_vma=False)
```

profile of v0, /device:TPU:1, one launch (start us, length us, event | category | flops | bytes accessed | tf_op | source)
XLA Modules:
  0.0 428.5 jit_solution(1268096922327915747)
XLA Ops:
  6.6 0.9 copy.54
  7.7 0.8 copy.58
  8.6 1.1 copy.57
  9.8 2.0 fusion.34
  12.2 0.7 copy.55
  13.1 0.6 reduce-window.6
  13.7 0.2 slice_reduce_fusion
  14.3 1.4 scatter_custom_fusion
  15.7 44.0 %all-gather.1 = f32[64,1,16]{2,1,0:T(1,128)S(1)} all-gather(f32[1,1,16]{2,1,0:T(1,128)S(1)} %get-tuple-element.60), channel_id=1, replica_groups=mesh['seq'=64,'tp'=4] {'seq'}, dimensions={0}, use_global_device_ids=true | all-gather | bytes 4160 | tf_op jit(solution)/shard_map/all_gather | solution.py:9
  59.8 0.6 iota_compare_fusion.2
  60.5 97.7 %all-gather.4.cloned.1.call-done = f32[1024,64,128]{2,1,0:T(8,128)} async-done(((f32[16,64,128]{2,1,0:T(8,128)}), f32[1024,64,128]{2,1,0:T(8,128)}) %all-gather.4.cloned.1.call-update) | async-done | bytes 33554448 | tf_op jit(solution)/shard_map/all_gather | solution.py:9
  158.3 1.2 while.12
  158.3 1.2 bitcast_add_fusion.2
  159.5 1.5 fusion.20
  161.1 2.3 multiply_reduce_fusion.1
  163.5 0.2 fusion.35
  163.7 1.5 convolution_convert_fusion.1
  165.4 117.4 %all-reduce.2.cloned.1.call-done = bf16[128,2048]{1,0:T(8,128)(2,1)} async-done(((bf16[128,2048]{1,0:T(8,128)(2,1)}), bf16[128,2048]{1,0:T(8,128)(2,1)}) %all-reduce.2.cloned.1.call-update) | async-done | bytes 524304 | tf_op jit(solution)/shard_map/psum | solution.py:106
  282.8 1.3 fusion.21
  284.1 0.2 fusion.23
  284.3 3.3 gather_fusion
  287.7 1.8 bitcast_select_fusion
  289.5 62.1 %all_to_all.10 = bf16[64,8,2048]{2,1,0:T(8,128)(2,1)S(1)} all-to-all(bf16[64,8,2048]{2,1,0:T(8,128)(2,1)S(1)} %bitcast_select_fusion), channel_id=1, replica_groups=mesh['seq'=64,'tp'=4] {'seq'}, dimensions={0} | all-to-all | bytes 4194304 | tf_op jit(solution)/shard_map/all_to_all | solution.py:113
  351.6 1.3 copy-done.2
  352.9 2.2 fusion.3
  355.1 6.3 %convolution_convert_fusion = bf16[512,2048]{1,0:T(8,128)(2,1)} fusion(bf16[1,512,2048]{2,1,0:T(8,128)(2,1)S(1)} %copy-done, bf16[1,2048,512]{2,1,0:T(8,128)(2,1)} %param.34, bf16[64,8,2048]{2,1,0:T(8,128)(2,1)} %copy-done.2, f32[512,512]{1,0:T(8,128)} %fusion.3), kind=kOutput, calls=%fused_computation.5 | convolution fusion | flops 2150105088 | bytes 9437184 | tf_op jit(solution)/shard_map/dot_general | solution.py:119
  361.4 29.5 %reduce-scatter.2.cloned.1.call-done = bf16[512,512]{1,0:T(8,128)(2,1)} async-done(((bf16[512,2048]{1,0:T(8,128)(2,1)}), bf16[512,512]{1,0:T(8,128)(2,1)}) %reduce-scatter.2.cloned.1.call-update) | async-done | bytes 524304 | tf_op jit(solution)/shard_map/reduce_scatter | solution.py:120
  390.9 10.6 %all-to-all-start.1 = ((bf16[64,8,512]{2,1,0:T(8,128)(2,1)}), bf16[64,8,512]{2,1,0:T(8,128)(2,1)S(1)}, u32[]{:S(2)}, u32[]{:S(2)}) async-start(bf16[64,8,512]{2,1,0:T(8,128)(2,1)} %bitcast.100), calls=%async_computation.2 | async-start | bytes 1048576 | tf_op jit(solution)/shard_map/all_to_all | solution.py:122
  402.0 17.2 %all-to-all-done.1 = bf16[64,8,512]{2,1,0:T(8,128)(2,1)S(1)} async-done(((bf16[64,8,512]{2,1,0:T(8,128)(2,1)}), bf16[64,8,512]{2,1,0:T(8,128)(2,1)S(1)}, u32[]{:S(2)}, u32[]{:S(2)}) %all-to-all-start.1) | async-done | bytes 524320 | tf_op jit(solution)/shard_map/all_to_all | solution.py:122
  419.2 1.2 gather_fusion.1
  420.4 0.8 multiply_reduce_fusion
  421.3 0.7 add_convert_fusion.1
  (75 shorter events, 2.4 us)
Async XLA Ops:
  6.5 348.6 %copy-start = (bf16[1,512,2048]{2,1,0:T(8,128)(2,1)S(1)}, bf16[1,512,2048]{2,1,0:T(8,128)(2,1)}, u32[]{:S(2)}) copy-start(bf16[1,512,2048]{2,1,0:T(8,128)(2,1)} %param.35) | copy-start | bytes 6291460
  6.5 53.8 %copy-start.5 = (bf16[128,128]{1,0:T(8,128)(2,1)S(1)}, bf16[128,128]{1,0:T(8,128)(2,1)}, u32[]{:S(2)}) copy-start(bf16[128,128]{1,0:T(8,128)(2,1)} %param.22) | copy-start | bytes 98308
  6.5 5.2 %copy-start.9 = (s32[128,2]{0,1:T(2,128)S(1)}, s32[128,2]{0,1:T(2,128)}, u32[]{:S(2)}) copy-start(s32[128,2]{0,1:T(2,128)} %param.31) | copy-start | bytes 3076
  6.5 6.4 %copy-start.4 = (bf16[128,1024]{1,0:T(8,128)(2,1)S(1)}, bf16[128,1024]{1,0:T(8,128)(2,1)}, u32[]{:S(2)}) copy-start(bf16[128,1024]{1,0:T(8,128)(2,1)} %param.21) | copy-start | bytes 786436
  6.5 53.8 %copy-start.6 = (bf16[128,128]{1,0:T(8,128)(2,1)S(1)}, bf16[128,128]{1,0:T(8,128)(2,1)}, u32[]{:S(2)}) copy-start(bf16[128,128]{1,0:T(8,128)(2,1)} %param.23) | copy-start | bytes 98308
  6.5 151.7 %all-gather.4.cloned.1.call-start = ((), (), s32[]{:S(2)}) async-start(), calls=%async_computation.5 | async-start | bytes 34078720 | tf_op jit(solution)/shard_map/all_gather | solution.py:9
  11.7 271.1 %all-reduce.2.cloned.1.call-start = ((), (), s32[]{:S(2)}) async-start(), calls=%async_computation.3 | async-start | bytes 1048576 | tf_op jit(solution)/shard_map/psum | solution.py:106
  14.3 45.4 %copy-start.7 = (s32[256]{0:T(256)}, s32[256]{0:T(256)S(1)}, u32[]{:S(2)}) copy-start(s32[256]{0:T(256)S(1)} %fusion.49) | copy-start | bytes 3076
  14.3 143.9 %copy-start.13 = (s32[256,1]{0,1:T(1,128)}, s32[256,1]{0,1:T(1,128)S(1)}, u32[]{:S(2)}) copy-start(s32[256,1]{0,1:T(1,128)S(1)} %compare_select_fusion) | copy-start | bytes 3076
  161.0 2.4 copy-start.12
  161.1 2.6 copy-start.1
  163.7 119.1 %copy-start.3 = (bf16[128,2048]{1,0:T(8,128)(2,1)S(1)}, bf16[128,2048]{1,0:T(8,128)(2,1)}, u32[]{:S(2)}) copy-start(bf16[128,2048]{1,0:T(8,128)(2,1)} %param.19) | copy-start | bytes 1572868
  165.2 118.9 %copy-start.11 = (f32[2048]{0:T(1024)S(1)}, f32[2048]{0:T(1024)}, u32[]{:S(2)}) copy-start(f32[2048]{0:T(1024)} %param.30) | copy-start | bytes 24580
  165.3 225.6 %reduce-scatter.2.cloned.1.call-start = ((), (), s32[]{:S(2)}) async-start(), calls=%async_computation.4 | async-start | bytes 2621440 | tf_op jit(solution)/shard_map/reduce_scatter | solution.py:120
  289.5 63.4 %copy-start.16 = (bf16[1,2048,512]{2,1,0:T(8,128)(2,1)S(1)}, bf16[1,2048,512]{2,1,0:T(8,128)(2,1)}, u32[]{:S(2)}) copy-start(bf16[1,2048,512]{2,1,0:T(8,128)(2,1)} %param.33) | copy-start | bytes 6291460
  351.6 1.3 copy-start.2
  361.4 40.1 %copy-start.8 = (s32[256]{0:T(256)S(1)}, s32[256]{0:T(256)}, u32[]{:S(2)}) copy-start(s32[256]{0:T(256)} %copy-done.7) | copy-start | bytes 3076
  361.4 40.3 %copy-start.10 = (s32[128,2]{0,1:T(2,128)S(1)}, s32[128,2]{0,1:T(2,128)}, u32[]{:S(2)}) copy-start(s32[128,2]{0,1:T(2,128)} %param.31) | copy-start | bytes 3076
  361.4 40.5 %copy-start.15 = (f32[128,2]{0,1:T(2,128)S(1)}, f32[128,2]{0,1:T(2,128)}, u32[]{:S(2)}) copy-start(f32[128,2]{0,1:T(2,128)} %param.32) | copy-start | bytes 3076
  361.4 40.6 %copy-start.14 = (s32[256,1]{0,1:T(1,128)S(1)}, s32[256,1]{0,1:T(1,128)}, u32[]{:S(2)}) copy-start(s32[256,1]{0,1:T(1,128)} %copy-done.13) | copy-start | bytes 3076
  390.9 28.3 %all-to-all-start.1 = ((bf16[64,8,512]{2,1,0:T(8,128)(2,1)}), bf16[64,8,512]{2,1,0:T(8,128)(2,1)S(1)}, u32[]{:S(2)}, u32[]{:S(2)}) async-start(bf16[64,8,512]{2,1,0:T(8,128)(2,1)} %bitcast.100), calls=%async_computation.2 | async-start | bytes 1048576 | tf_op jit(solution)/shard_map/all_to_all | solution.py:122
Sparse Core Ops, SparseCore 0:
  11.8 146.3 all-gather.3
  165.4 117.3 all-reduce.1
  361.5 29.3 reduce-scatter.1
where the time goes:
time: 432 us; the launch traced here: 429 us
  waiting for transfers between devices  262 us (61%)
  blocking collectives  106 us (25%)
  matrix products  15.9 us (4%)
  between operations  13.5 us (3%)
  local copies, waits for them, and re-layouts  12.6 us (3%)
  starting transfers between devices  10.7 us (2%)
  other arithmetic  7.94 us (2%)
    psum x1, waiting for transfers between devices, body(): lax.psum(partial_value.astype(jnp.bfloat16), 'tp').astype(jnp.float32)  117 us
    all_gather x1, waiting for transfers between devices, entering(): gathered = jax.tree.map(lambda a: lax.all_gather(a, axis), part)  97.7 us
    all_to_all x1, blocking collectives, body(): lax.all_to_all(outgoing, 'seq', split_axis=0, concat_axis=0, tiled=True)  62.1 us
    all_gather x1, blocking collectives, entering(): gathered = jax.tree.map(lambda a: lax.all_gather(a, axis), part)  44 us
    reduce_scatter x1, waiting for transfers between devices, body(): lax.psum_scatter(down_val.astype(jnp.bfloat16), 'tp', scatter_dimension=1...  29.5 us
    all_to_all x1, waiting for transfers between devices, body(): lax.all_to_all(results, 'seq', split_axis=0, concat_axis=0, tiled=True)  17.2 us
    all_to_all x1, starting transfers between devices, body(): lax.all_to_all(results, 'seq', split_axis=0, concat_axis=0, tiled=True)  10.6 us
  transfers between devices with their start and end apart: 4, of which 4 were waited for; matrix products, arithmetic and copies ran while one was open for 1% of the time, Pallas kernels for 0%

commit v1 on v0

v1 whole, which is shorter than its diff:
```python
import functools

import jax
import jax.numpy as jnp
from jax import lax
from jax.experimental import pallas as pl
from jax.experimental.pallas import tpu as pltpu
from jax.sharding import PartitionSpec as P

F32 = jnp.float32
BF16 = jnp.bfloat16
HI = lax.Precision.HIGHEST
MESH = pl.DeviceIdType.MESH
NZ, NX, NC = 8, 4, 2
NS = NZ * NX * NC
NY = 4
TOK = 128
HEADS = 16
INNER = 1024
WIDTH = 2048
SLICE = 512
SLOTS = 8
GROUPS = 4
GS = NS // GROUPS


def shifted(me, i, sign):
    z, x, c = me // 8, lax.rem(me // 2, 4), lax.rem(me, 2)
    dz, dx, dc = i // 8, lax.rem(i // 2, 4), lax.rem(i, 2)
    z2 = lax.rem(z + NZ + sign * dz, NZ)
    x2 = lax.rem(x + NX + sign * dx, NX)
    c2 = lax.rem(c + NC + sign * dc, NC)
    return z2 * 8 + x2 * 2 + c2


def iota(shape, dim):
    return lax.broadcasted_iota(jnp.int32, shape, dim)


def mm(a, b):
    return jnp.dot(a, b, preferred_element_type=F32)


def mm_nt(a, b, precision=None):
    return lax.dot_general(a, b, (((1,), (1,)), ((), ())), precision=precision, preferred_element_type=F32)


def split2(v):
    hi = v.astype(BF16)
    return hi, (v - hi.astype(F32)).astype(BF16)


def split3(v):
    hi, mid = split2(v)
    low = (v - hi.astype(F32) - mid.astype(F32)).astype(BF16)
    return hi, mid, low


def kernel(
    x_ref, z_ref, b_ref, c_ref, dt_ref, la_ref, skip_ref, ngain_ref, mgain_ref, routes_ref, rw_ref,
    tokens_hbm, init_hbm, wout_hbm, wg_hbm, wu_hbm, wd_hbm,
    out_ref,
    msg1, recv1, res, recv2, ybuf, szbuf, expcum, normed,
    tok_v, init_v, wout_v, wg_v, wu_v, wd_v,
    disp, xs, accg, accu, hid, wts,
    far_s, far_r, near_s, near_r, pbuf, rets, retr,
    wsem, s1, r1, s2, r2, sd, rd, sr, rr, ag_s, ag_r, rs_s, rs_r,
):
    me = lax.axis_index("seq")
    y = lax.axis_index("tp")
    up_y = lax.rem(y + 1, NY)
    dn_y = lax.rem(y + NY - 1, NY)
    far_y = lax.rem(y + 2, NY)

    barrier = pltpu.get_barrier_semaphore()

    def greet(i, carry):
        pl.semaphore_signal(barrier, inc=1, device_id=(shifted(me, i, 1), y), device_id_type=MESH)
        return carry

    lax.fori_loop(1, NS, greet, 0)
    for peer in (up_y, dn_y):
        pl.semaphore_signal(barrier, inc=1, device_id=(me, peer), device_id_type=MESH)

    own_col = pl.multiple_of(y * SLICE, SLICE)
    tile_row = pl.multiple_of((me // 8) * 128, 128)
    loads = [
        pltpu.make_async_copy(init_hbm.at[pl.ds(tile_row, 128), :], init_v, wsem.at[0]),
        pltpu.make_async_copy(tokens_hbm.at[:, pl.ds(own_col, SLICE)], tok_v, wsem.at[1]),
        pltpu.make_async_copy(wout_hbm, wout_v, wsem.at[2]),
        pltpu.make_async_copy(wg_hbm, wg_v, wsem.at[3]),
        pltpu.make_async_copy(wu_hbm, wu_v, wsem.at[4]),
        pltpu.make_async_copy(wd_hbm, wd_v, wsem.at[5]),
    ]
    for load in loads:
        load.start()

    rows = iota((TOK, TOK), 0)
    cols = iota((TOK, TOK), 1)
    causal = (rows >= cols).astype(F32)
    eye = (rows == cols).astype(BF16)
    dt = dt_ref[...]
    cum = jnp.dot(causal, la_ref[...], precision=HI, preferred_element_type=F32)
    end = cum[TOK - 1 : TOK, :]
    expand = (iota((HEADS, INNER), 1) // 64 == iota((HEADS, INNER), 0)).astype(BF16)
    w_hi, w_lo = split2(jnp.exp(end - cum) * dt)
    w_wide = mm(w_hi, expand) + mm(w_lo, expand)
    x_wide = x_ref[...].astype(F32)
    xw = (x_wide * w_wide).astype(BF16)
    d3 = split3(jnp.exp(end))
    k3 = split3(skip_ref[...])
    r8 = iota((8, HEADS), 0)
    small = jnp.zeros((8, HEADS), F32)
    for n, part in enumerate(d3 + k3):
        small = jnp.where(r8 == n, part.astype(F32), small)
    small_wide = mm(small.astype(BF16), expand)
    b_t = mm_nt(eye, b_ref[...]).astype(BF16)
    state_t = mm(b_t, xw)
    small_bf = small_wide.astype(BF16)
    for l in range(8):
        lanes = slice(l * 128, (l + 1) * 128)
        msg1[l * 8 : (l + 1) * 8, 0:16, :] = state_t[:, lanes].astype(BF16).reshape(8, 16, 128)
        msg1[l * 8 : (l + 1) * 8, 16:24, :] = jnp.broadcast_to(small_bf[None, :, lanes], (8, 8, 128))

    pl.semaphore_wait(barrier, NS - 1 + 2)

    def send1(i, carry):
        q = shifted(me, i, 1)
        pltpu.make_async_remote_copy(
            src_ref=msg1.at[q], dst_ref=recv1.at[me], send_sem=s1, recv_sem=r1,
            device_id=(q, y), device_id_type=MESH,
        ).start()
        return carry

    lax.fori_loop(1, NS, send1, 0)
    recv1[pl.ds(me, 1)] = msg1[pl.ds(me, 1)]

    e_hi, e_lo = split2(jnp.exp(cum))
    expcum[...] = mm(e_hi, expand) + mm(e_lo, expand)
    eye16 = (iota((HEADS, HEADS), 0) == iota((HEADS, HEADS), 1)).astype(F32)
    cum_t = mm_nt(eye16, cum, HI)
    dt_t = mm_nt(eye16, dt, HI)
    scores = mm_nt(c_ref[...], b_ref[...]) * causal
    low_half = (iota((TOK, 128), 1) < 64).astype(F32)
    skip_wide = small_wide[3:4, :] + small_wide[4:5, :] + small_wide[5:6, :]
    for l in range(8):
        lanes = slice(l * 128, (l + 1) * 128)
        mixes = []
        for h in (2 * l, 2 * l + 1):
            gap = jnp.minimum(cum[:, h : h + 1] - cum_t[h : h + 1, :], 0.0)
            mixes.append((jnp.exp(gap) * scores * dt_t[h : h + 1, :]).astype(BF16))
        x_l = x_wide[:, lanes]
        x_lo = x_l * low_half
        rhs = jnp.concatenate([x_lo.astype(BF16), (x_l - x_lo).astype(BF16)], axis=0)
        ybuf[:, lanes] = mm(jnp.concatenate(mixes, axis=1), rhs) + skip_wide[:, lanes] * x_l
        z_l = z_ref[:, lanes].astype(F32)
        szbuf[:, lanes] = 0.5 * z_l * (1.0 + jnp.tanh(0.5 * z_l))

    sel2 = (iota((8, 2), 0) == iota((8, 2), 1)).astype(F32)
    routes_t = mm_nt(sel2, routes_ref[...].astype(F32), HI).astype(jnp.int32)
    rw_t = mm_nt(sel2, rw_ref[...], HI)
    zme, xme, cme = me // 8, lax.rem(me // 2, 4), lax.rem(me, 2)
    off = (
        (((routes_t >> 3) - zme + 8) & 7) * 8
        + ((((routes_t >> 1) & 3) - xme + 4) & 3) * 2
        + (((routes_t & 1) - cme + 2) & 1)
    )
    place = iota((NS, TOK), 0)
    first = off[0:1, :] == place
    second = off[1:2, :] == place
    named = jnp.where(first, 1.0, 0.0) + jnp.where(second, 1.0, 0.0)
    weight = jnp.where(first, rw_t[0:1, :], 0.0) + jnp.where(second, rw_t[1:2, :], 0.0)
    before = (rows < cols).astype(BF16)
    rank = mm(named.astype(BF16), before)
    rank = jnp.where(named > 0.5, rank, -1.0)
    slot_id = iota((NS, SLOTS, TOK), 1).astype(F32)
    hit = jnp.broadcast_to(rank[:, None, :], (NS, SLOTS, TOK)) == slot_id
    pick = jnp.where(hit, 1.0, 0.0).reshape(NS * SLOTS, TOK).astype(BF16)
    pick_w = jnp.where(hit, jnp.broadcast_to(weight[:, None, :], (NS, SLOTS, TOK)), 0.0).reshape(NS * SLOTS, TOK)
    pw_hi, pw_lo = split2(pick_w)
    wts[0] = mm_nt(eye, pw_hi).astype(BF16)
    wts[1] = mm_nt(eye, pw_lo).astype(BF16)

    loads[0].wait()
    row0 = lax.rem(me, 8) * 16
    sel16 = (iota((16, 128), 1) == iota((16, 128), 0) + row0).astype(F32)
    start = mm_nt(sel16, init_v[...], HI)
    pltpu.make_async_remote_copy(
        src_ref=recv1.at[pl.ds(0, NS - 1)], dst_ref=recv1.at[pl.ds(0, NS - 1)], send_sem=s1, recv_sem=r1,
        device_id=(me, up_y), device_id_type=MESH,
    ).wait_recv()

    def step(p, state):
        res[p] = state.astype(BF16)
        piece = recv1[p].astype(F32)
        decay = piece[16:17, :] + piece[17:18, :] + piece[18:19, :]
        return decay * state + piece[0:16, :]

    lax.fori_loop(0, NS, step, start)

    def send2(i, carry):
        q = shifted(me, i, 1)
        pltpu.make_async_remote_copy(
            src_ref=res.at[q], dst_ref=recv2.at[me], send_sem=s2, recv_sem=r2,
            device_id=(q, y), device_id_type=MESH,
        ).start()
        return carry

    lax.fori_loop(1, NS, send2, 0)
    recv2[pl.ds(me, 1)] = res[pl.ds(me, 1)]
    pltpu.make_async_remote_copy(
        src_ref=recv2.at[pl.ds(0, NS - 1)], dst_ref=recv2.at[pl.ds(0, NS - 1)], send_sem=s2, recv_sem=r2,
        device_id=(me, up_y), device_id_type=MESH,
    ).wait_recv()

    same_head = (iota((128, 128), 0) // 64 == iota((128, 128), 1) // 64).astype(BF16)
    c_bf = c_ref[...]
    for l in range(8):
        lanes = slice(l * 128, (l + 1) * 128)
        entering = recv2[l * 8 : (l + 1) * 8].reshape(128, 128)
        v = ybuf[:, lanes] + mm(c_bf, entering) * expcum[:, lanes]
        v = v * szbuf[:, lanes]
        mean_sq = mm((v * v).astype(BF16), same_head) * (1.0 / 64.0)
        normed[:, lanes] = (v * lax.rsqrt(mean_sq + 1e-05) * ngain_ref[:, lanes]).astype(BF16)

    def rs_copy(n, k):
        sent, landed, side = (far_s, far_r, k) if k < 2 else (near_s, near_r, k - 2)
        return pltpu.make_async_remote_copy(
            src_ref=sent.at[n, side], dst_ref=landed.at[n, side],
            send_sem=rs_s.at[n, k], recv_sem=rs_r.at[n, k],
            device_id=(me, dn_y if side else up_y), device_id_type=MESH,
        )

    half = TOK // 2

    def rs_begin(n, lhs, w_v):
        part = mm(lhs, w_v[:, pl.ds(pl.multiple_of(far_y * SLICE, SLICE), SLICE)]).astype(BF16)
        far_s[n, 0] = part[:half]
        far_s[n, 1] = part[half:]
        rs_copy(n, 0).start()
        rs_copy(n, 1).start()
        for slot, where in ((0, up_y), (1, dn_y), (2, y)):
            pbuf[n, slot] = mm(lhs, w_v[:, pl.ds(pl.multiple_of(where * SLICE, SLICE), SLICE)])

    def rs_middle(n):
        rs_copy(n, 0).wait_recv()
        near_s[n, 0, :half] = (pbuf[n, 0, :half] + far_r[n, 0].astype(F32)).astype(BF16)
        near_s[n, 0, half:] = pbuf[n, 0, half:].astype(BF16)
        rs_copy(n, 2).start()
        rs_copy(n, 1).wait_recv()
        near_s[n, 1, :half] = pbuf[n, 1, :half].astype(BF16)
        near_s[n, 1, half:] = (pbuf[n, 1, half:] + far_r[n, 1].astype(F32)).astype(BF16)
        rs_copy(n, 3).start()

    def rs_end(n):
        rs_copy(n, 2).wait_recv()
        rs_copy(n, 3).wait_recv()
        return pbuf[n, 2] + near_r[n, 0].astype(F32) + near_r[n, 1].astype(F32)

    loads[2].wait()
    rs_begin(GROUPS, normed[...], wout_v)
    loads[1].wait()
    rs_middle(GROUPS)
    hidden = (tok_v[...].astype(F32) + rs_end(GROUPS)).astype(BF16)
    hid[...] = hidden
    disp[...] = mm(pick, hidden).astype(BF16).reshape(NS, SLOTS, SLICE)

    for g in range(GROUPS):
        def send_d(i, carry):
            pltpu.make_async_remote_copy(
                src_ref=disp.at[i], dst_ref=xs.at[0, i], send_sem=sd, recv_sem=rd.at[g],
                device_id=(shifted(me, i, 1), y), device_id_type=MESH,
            ).start()
            return carry

        lax.fori_loop(max(1, g * GS), (g + 1) * GS, send_d, 0)
    xs[0, 0] = disp[0]
    for load in loads[3:]:
        load.wait()

    def ag_copy(g, k):
        src, dst, first, count, peer = (
            (0, 1, 0, GS, up_y),
            (0, 3, 0, GS, dn_y),
            (1, 2, 0, GS // 2, up_y),
            (3, 2, GS // 2, GS // 2, dn_y),
        )[k]
        part = pl.ds(g * GS + first, count)
        return pltpu.make_async_remote_copy(
            src_ref=xs.at[src, part], dst_ref=xs.at[dst, part],
            send_sem=ag_s.at[g, k], recv_sem=ag_r.at[g, k], device_id=(me, peer), device_id_type=MESH,
        )

    def arrive(g):
        count = GS - 1 if g == 0 else GS
        part = xs.at[0, pl.ds((g + 1) * GS - count, count)]
        pltpu.make_async_remote_copy(
            src_ref=part, dst_ref=part, send_sem=sd, recv_sem=rd.at[g], device_id=(me, up_y), device_id_type=MESH,
        ).wait_recv()
        ag_copy(g, 0).start()
        ag_copy(g, 1).start()

    def forward(g):
        ag_copy(g, 0).wait_recv()
        ag_copy(g, 2).start()
        ag_copy(g, 1).wait_recv()
        ag_copy(g, 3).start()

    def expert(g):
        ag_copy(g, 2).wait_recv()
        ag_copy(g, 3).wait_recv()
        accg[...] = jnp.zeros_like(accg)
        accu[...] = jnp.zeros_like(accu)

        def piece(o, total):
            owner = lax.rem(y + NY - o, NY)
            at = pl.multiple_of(owner * SLICE, SLICE)
            v = xs[o, pl.ds(g * GS, GS)].astype(F32).reshape(TOK, SLICE)
            vg = (v * mgain_ref[:, pl.ds(at, SLICE)]).astype(BF16)
            accg[...] += mm(vg, wg_v[pl.ds(at, SLICE), :])
            accu[...] += mm(vg, wu_v[pl.ds(at, SLICE), :])
            return total + jnp.sum(v * v, axis=1, keepdims=True)

        total = lax.fori_loop(0, NY, piece, jnp.zeros((TOK, 1), F32))
        scale = lax.rsqrt(total * (1.0 / WIDTH) + 1e-05)
        gate = accg[...] * scale
        act = (0.5 * gate * (1.0 + jnp.tanh(0.5 * gate)) * (accu[...] * scale)).astype(BF16)
        rs_begin(g, act, wd_v)

    def give_back(g):
        rets[g * GS : (g + 1) * GS] = rs_end(g).astype(BF16).reshape(GS, SLOTS, SLICE)

        def send_r(i, carry):
            pltpu.make_async_remote_copy(
                src_ref=rets.at[i], dst_ref=retr.at[i], send_sem=sr, recv_sem=rr.at[g],
                device_id=(shifted(me, i, -1), y), device_id_type=MESH,
            ).start()
            return carry

        lax.fori_loop(max(1, g * GS), (g + 1) * GS, send_r, 0)

    stages = (arrive, forward, expert, rs_middle, give_back)
    for k in range(GROUPS + len(stages) - 1):
        for n, stage in enumerate(stages):
            if 0 <= k - n < GROUPS:
                stage(k - n)

    retr[0] = rets[0]
    total = hid[...].astype(F32)
    for g in range(GROUPS):
        count = GS - 1 if g == 0 else GS
        part = retr.at[pl.ds((g + 1) * GS - count, count)]
        pltpu.make_async_remote_copy(
            src_ref=part, dst_ref=part, send_sem=sr, recv_sem=rr.at[g], device_id=(me, up_y), device_id_type=MESH,
        ).wait_recv()
        back = retr[g * GS : (g + 1) * GS].reshape(TOK, SLICE)
        lanes = slice(g * TOK, (g + 1) * TOK)
        total = total + mm(wts[0, :, lanes], back) + mm(wts[1, :, lanes], back)
    out_ref[...] = total.astype(BF16)

    for buf, sem in ((msg1, s1), (res, s2), (disp, sd), (rets, sr)):
        part = buf.at[pl.ds(0, NS - 1)]
        pltpu.make_async_remote_copy(
            src_ref=part, dst_ref=part, send_sem=sem, recv_sem=r1, device_id=(me, up_y), device_id_type=MESH,
        ).wait_send()
    for g in range(GROUPS):
        for k in range(4):
            ag_copy(g, k).wait_send()
    for n in range(GROUPS + 1):
        for k in range(4):
            rs_copy(n, k).wait_send()


def body(
    tokens, input_heads, z_gate, b_proj, c_proj, step_size, decay_log, skip_gain, init_state, norm_gain,
    out_weight, moe_gain, routes, route_weights, w_gate, w_up, w_down,
):
    vmem = pl.BlockSpec(memory_space=pltpu.VMEM)
    hbm = pl.BlockSpec(memory_space=pl.ANY)
    dma = pltpu.SemaphoreType.DMA
    n = GROUPS + 1
    scratch = [
        pltpu.VMEM((NS, 24, 128), BF16),
        pltpu.VMEM((NS, 24, 128), BF16),
        pltpu.VMEM((NS, 16, 128), BF16),
        pltpu.VMEM((NS, 16, 128), BF16),
        pltpu.VMEM((TOK, INNER), F32),
        pltpu.VMEM((TOK, INNER), F32),
        pltpu.VMEM((TOK, INNER), F32),
        pltpu.VMEM((TOK, INNER), BF16),
        pltpu.VMEM((TOK, SLICE), BF16),
        pltpu.VMEM((128, 128), F32),
        pltpu.VMEM((INNER, WIDTH), BF16),
        pltpu.VMEM((WIDTH, SLICE), BF16),
        pltpu.VMEM((WIDTH, SLICE), BF16),
        pltpu.VMEM((SLICE, WIDTH), BF16),
        pltpu.VMEM((NS, SLOTS, SLICE), BF16),
        pltpu.VMEM((NY, NS, SLOTS, SLICE), BF16),
        pltpu.VMEM((TOK, SLICE), F32),
        pltpu.VMEM((TOK, SLICE), F32),
        pltpu.VMEM((TOK, SLICE), BF16),
        pltpu.VMEM((2, TOK, NS * SLOTS), BF16),
        pltpu.VMEM((n, 2, TOK // 2, SLICE), BF16),
        pltpu.VMEM((n, 2, TOK // 2, SLICE), BF16),
        pltpu.VMEM((n, 2, TOK, SLICE), BF16),
        pltpu.VMEM((n, 2, TOK, SLICE), BF16),
        pltpu.VMEM((n, 3, TOK, SLICE), F32),
        pltpu.VMEM((NS, SLOTS, SLICE), BF16),
        pltpu.VMEM((NS, SLOTS, SLICE), BF16),
        dma((6,)),
        dma, dma, dma, dma,
        dma, dma((GROUPS,)),
        dma, dma((GROUPS,)),
        dma((GROUPS, 4)), dma((GROUPS, 4)),
        dma((n, 4)), dma((n, 4)),
    ]
    return pl.pallas_call(
        kernel,
        out_shape=jax.ShapeDtypeStruct((TOK, SLICE), BF16),
        in_specs=[vmem] * 11 + [hbm] * 6,
        out_specs=vmem,
        scratch_shapes=scratch,
        name="mixer_moe",
        compiler_params=pltpu.CompilerParams(
            collective_id=0, has_side_effects=True, vmem_limit_bytes=56 * 1024 * 1024
        ),
    )(
        input_heads, z_gate, b_proj, c_proj, step_size, decay_log, skip_gain.reshape(1, HEADS),
        norm_gain.reshape(1, INNER), moe_gain.reshape(1, WIDTH), routes, route_weights,
        tokens, init_state.reshape(INNER, 128), out_weight, w_gate[0], w_up[0], w_down[0],
    )


def solution(mesh):
    in_specs = (
        P("seq", None),
        P("seq", "tp"),
        P("seq", "tp"),
        P("seq", None),
        P("seq", None),
        P("seq", "tp"),
        P("seq", "tp"),
        P("tp"),
        P("tp", None, None),
        P("tp"),
        P("tp", None),
        P(),
        P("seq", None),
        P("seq", None),
        P("seq", None, "tp"),
        P("seq", None, "tp"),
        P("seq", "tp", None),
    )
    return jax.shard_map(body, mesh=mesh, in_specs=in_specs, out_specs=P("seq", "tp"), check_vma=False)
```

time: 432 us -> 114 us (0.26)
  waiting for transfers between devices: 262 us -> 0 us
  Pallas kernels: 0 us -> 107 us
  blocking collectives: 106 us -> 0 us
  matrix products: 15.9 us -> 0 us
  between operations: 13.5 us -> 0.01 us
  starting transfers between devices: 10.7 us -> 0 us
  other arithmetic: 7.94 us -> 0 us
  local copies, waits for them, and re-layouts: 12.6 us -> 7.21 us
    psum x1 -> x0, waiting for transfers between devices: 117 us -> none  [body(): lax.psum(partial_value.astype(jnp.bfloat16), 'tp').astype(jnp.float32)]
    pallas_call x0 -> x1, Pallas kernels: none -> 107 us  [body(): pl.pallas_call(kernel, out_shape=jax.ShapeDtypeStruct((TOK, SLICE), BF16)...]
    all_gather x1 -> x0, waiting for transfers between devices: 97.7 us -> none  [entering(): gathered = jax.tree.map(lambda a: lax.all_gather(a, axis), part)]
    all_to_all x1 -> x0, blocking collectives: 62.1 us -> none  [body(): lax.all_to_all(outgoing, 'seq', split_axis=0, concat_axis=0, tiled=True)]
    all_gather x1 -> x0, blocking collectives: 44 us -> none  [entering(): gathered = jax.tree.map(lambda a: lax.all_gather(a, axis), part)]
    reduce_scatter x1 -> x0, waiting for transfers between devices: 29.5 us -> none  [body(): lax.psum_scatter(down_val.astype(jnp.bfloat16), 'tp', scatter_dimension=1...]
    all_to_all x1 -> x0, waiting for transfers between devices: 17.2 us -> none  [body(): lax.all_to_all(results, 'seq', split_axis=0, concat_axis=0, tiled=True)]
    dot_general x7 -> x0, matrix products: 15.9 us -> none  [the longest x1 6.25 us: body(): down_val = jnp.dot(act_vals, w_down[0], preferred_element_type=jnp.float32)]
  transfers between devices with their start and end apart: 4 -> 0, of which waited for: 4 -> 0; matrix products, arithmetic and copies ran while one was open for 1% -> 0% of each run, Pallas kernels for 0% -> 0%
where the time goes in v1:
time: 114 us
  Pallas kernels  107 us (94%)
  local copies, waits for them, and re-layouts  7.21 us (6%)
    pallas_call x1, Pallas kernels, body(): pl.pallas_call(kernel, out_shape=jax.ShapeDtypeStruct((TOK, SLICE), BF16)...  107 us
    unnamed x5, local copies, waits for them, and re-layouts  7.21 us

profile of v1, /device:TPU:1, one launch (start us, length us, event | category | flops | bytes accessed | tf_op | source)
XLA Modules:
  0.0 113.8 jit_solution(15759844728964323257)
XLA Ops:
  0.0 1.4 %copy.18.dt_ref = f32[128,16]{1,0:T(8,128)} copy(f32[128,16]{0,1:T(8,128)} %param.22) | data formatting | bytes 16384 | tf_op args[5]
  1.4 1.4 %copy.19.la_ref = f32[128,16]{1,0:T(8,128)} copy(f32[128,16]{0,1:T(8,128)} %param.23) | data formatting | bytes 16384 | tf_op args[6]
  2.8 1.4 %copy.20.routes_ref = s32[128,2]{1,0:T(8,128)} copy(s32[128,2]{0,1:T(2,128)} %param.29) | data formatting | bytes 2048 | tf_op args[12]
  4.2 1.4 %copy.21.rw_ref = f32[128,2]{1,0:T(8,128)} copy(f32[128,2]{0,1:T(2,128)} %param.30) | data formatting | bytes 2048 | tf_op args[13]
  5.6 106.5 %mixer_moe.1 = bf16[128,512]{1,0:T(8,128)(2,1)} custom-call(bf16[128,1024]{1,0:T(8,128)(2,1)} %x_ref.1, bf16[128,1024]{1,0:T(8,128)(2,1)} %z_ref.1, bf16[128,128]{1,0:T(8,128)(2,1)} %b_ref.1, bf16[128,128]{1,0:T(8,128)(2,1)} %c_ref.1, f32[128,16]{1,0:T(8,128)} %copy.18.dt_ref, f32[128,16]{1,0:T(8,128)} %copy.19.la_ref, f32[1,16]{1,0:T(1,128)} %bitcast.13, ...), custom_call_target="tpu_custom_call" | custom-call | tf_op jit(solution)/shard_map/mixer_moe/pallas_call | solution.py:417
  112.2 1.6 %copy.23 = bf16[128,512]{1,0:T(8,128)(2,1)} copy(bf16[128,512]{1,0:T(8,128)(2,1)} %mixer_moe.1) | data formatting | bytes 262144

commit v2 on v1

--- a/solution.py
+++ b/solution.py
@@ -13,6 +13,7 @@
 MESH = pl.DeviceIdType.MESH
 NZ, NX, NC = 8, 4, 2
 NS = NZ * NX * NC
+NP = NX * NC
 NY = 4
 TOK = 128
 HEADS = 16
@@ -22,6 +23,8 @@
 SLOTS = 8
 GROUPS = 4
 GS = NS // GROUPS
+DZ = (1, 7, 2, 6, 0, 4, 3, 5)
+OWN = DZ.index(0) * NP
 
 
 def shifted(me, i, sign):
@@ -60,11 +63,11 @@
     x_ref, z_ref, b_ref, c_ref, dt_ref, la_ref, skip_ref, ngain_ref, mgain_ref, routes_ref, rw_ref,
     tokens_hbm, init_hbm, wout_hbm, wg_hbm, wu_hbm, wd_hbm,
     out_ref,
-    msg1, recv1, res, recv2, ybuf, szbuf, expcum, normed,
+    msg1, recv1, msg2, recv2, msg3, recv3, msg4, recv4, inner, through, ybuf, szbuf, expcum, normed,
     tok_v, init_v, wout_v, wg_v, wu_v, wd_v,
     disp, xs, accg, accu, hid, wts,
     far_s, far_r, near_s, near_r, pbuf, rets, retr,
-    wsem, s1, r1, s2, r2, sd, rd, sr, rr, ag_s, ag_r, rs_s, rs_r,
+    wsem, xsem_s, xsem_r, sd, rd, sr, rr, ag_s, ag_r, rs_s, rs_r,
 ):
     me = lax.axis_index("seq")
     y = lax.axis_index("tp")
@@ -78,12 +81,14 @@
         pl.semaphore_signal(barrier, inc=1, device_id=(shifted(me, i, 1), y), device_id_type=MESH)
         return carry
 
-    lax.fori_loop(1, NS, greet, 0)
+    lax.fori_loop(1, NP, greet, 0)
+    lax.fori_loop(1, NZ, lambda i, carry: greet(i * NP, carry), 0)
     for peer in (up_y, dn_y):
         pl.semaphore_signal(barrier, inc=1, device_id=(me, peer), device_id_type=MESH)
 
     own_col = pl.multiple_of(y * SLICE, SLICE)
-    tile_row = pl.multiple_of((me // 8) * 128, 128)
+    plane, spot = me // NP, lax.rem(me, NP)
+    tile_row = pl.multiple_of(spot * 128, 128)
     loads = [
         pltpu.make_async_copy(init_hbm.at[pl.ds(tile_row, 128), :], init_v, wsem.at[0]),
         pltpu.make_async_copy(tokens_hbm.at[:, pl.ds(own_col, SLICE)], tok_v, wsem.at[1]),
@@ -99,8 +104,11 @@
     cols = iota((TOK, TOK), 1)
     causal = (rows >= cols).astype(F32)
     eye = (rows == cols).astype(BF16)
-    dt = dt_ref[...]
-    cum = jnp.dot(causal, la_ref[...], precision=HI, preferred_element_type=F32)
+    eye_f = eye.astype(F32)
+    dt_t = dt_ref[...]
+    cum_t = mm_nt(la_ref[...], causal, HI)
+    cum = mm_nt(eye_f, cum_t, HI)
+    dt = mm_nt(eye_f, dt_t, HI)
     end = cum[TOK - 1 : TOK, :]
     expand = (iota((HEADS, INNER), 1) // 64 == iota((HEADS, INNER), 0)).astype(BF16)
     w_hi, w_lo = split2(jnp.exp(end - cum) * dt)
@@ -116,30 +124,39 @@
     small_wide = mm(small.astype(BF16), expand)
     b_t = mm_nt(eye, b_ref[...]).astype(BF16)
     state_t = mm(b_t, xw)
-    small_bf = small_wide.astype(BF16)
-    for l in range(8):
+    small_bf = jnp.concatenate([small_wide, small_wide], axis=0).astype(BF16)
+    for l in range(NP):
         lanes = slice(l * 128, (l + 1) * 128)
-        msg1[l * 8 : (l + 1) * 8, 0:16, :] = state_t[:, lanes].astype(BF16).reshape(8, 16, 128)
-        msg1[l * 8 : (l + 1) * 8, 16:24, :] = jnp.broadcast_to(small_bf[None, :, lanes], (8, 8, 128))
-
-    pl.semaphore_wait(barrier, NS - 1 + 2)
-
-    def send1(i, carry):
-        q = shifted(me, i, 1)
-        pltpu.make_async_remote_copy(
-            src_ref=msg1.at[q], dst_ref=recv1.at[me], send_sem=s1, recv_sem=r1,
-            device_id=(q, y), device_id_type=MESH,
-        ).start()
-        return carry
-
-    lax.fori_loop(1, NS, send1, 0)
-    recv1[pl.ds(me, 1)] = msg1[pl.ds(me, 1)]
+        msg1[l, 0:128, :] = state_t[:, lanes].astype(BF16)
+        msg1[l, 128:144, :] = small_bf[:, lanes]
+
+    pl.semaphore_wait(barrier, NP - 1 + NZ - 1 + 2)
+
+    def exchange(sent, landed, send_sem, recv_sem, across):
+        mine = plane if across else spot
+
+        def one(i, carry):
+            q = shifted(me, i * NP if across else i, 1)
+            pltpu.make_async_remote_copy(
+                src_ref=sent.at[q // NP if across else lax.rem(q, NP)], dst_ref=landed.at[mine],
+                send_sem=send_sem, recv_sem=recv_sem, device_id=(q, y), device_id_type=MESH,
+            ).start()
+            return carry
+
+        lax.fori_loop(1, NP, one, 0)
+        landed[pl.ds(mine, 1)] = sent[pl.ds(mine, 1)]
+
+    def exchanged(landed, send_sem, recv_sem):
+        part = landed.at[pl.ds(0, NP - 1)]
+        return pltpu.make_async_remote_copy(
+            src_ref=part, dst_ref=part, send_sem=send_sem, recv_sem=recv_sem,
+            device_id=(me, up_y), device_id_type=MESH,
+        )
+
+    exchange(msg1, recv1, xsem_s.at[0], xsem_r.at[0], False)
 
     e_hi, e_lo = split2(jnp.exp(cum))
     expcum[...] = mm(e_hi, expand) + mm(e_lo, expand)
-    eye16 = (iota((HEADS, HEADS), 0) == iota((HEADS, HEADS), 1)).astype(F32)
-    cum_t = mm_nt(eye16, cum, HI)
-    dt_t = mm_nt(eye16, dt, HI)
     scores = mm_nt(c_ref[...], b_ref[...]) * causal
     low_half = (iota((TOK, 128), 1) < 64).astype(F32)
     skip_wide = small_wide[3:4, :] + small_wide[4:5, :] + small_wide[5:6, :]
@@ -156,15 +173,14 @@
         z_l = z_ref[:, lanes].astype(F32)
         szbuf[:, lanes] = 0.5 * z_l * (1.0 + jnp.tanh(0.5 * z_l))
 
-    sel2 = (iota((8, 2), 0) == iota((8, 2), 1)).astype(F32)
-    routes_t = mm_nt(sel2, routes_ref[...].astype(F32), HI).astype(jnp.int32)
-    rw_t = mm_nt(sel2, rw_ref[...], HI)
+    routes_t = routes_ref[...]
+    rw_t = rw_ref[...]
     zme, xme, cme = me // 8, lax.rem(me // 2, 4), lax.rem(me, 2)
-    off = (
-        (((routes_t >> 3) - zme + 8) & 7) * 8
-        + ((((routes_t >> 1) & 3) - xme + 4) & 3) * 2
-        + (((routes_t & 1) - cme + 2) & 1)
-    )
+    dz = ((routes_t >> 3) - zme + 8) & 7
+    group = jnp.zeros_like(dz)
+    for n, value in enumerate(DZ):
+        group = jnp.where(dz == value, n, group)
+    off = group * 8 + ((((routes_t >> 1) & 3) - xme + 4) & 3) * 2 + (((routes_t & 1) - cme + 2) & 1)
     place = iota((NS, TOK), 0)
     first = off[0:1, :] == place
     second = off[1:2, :] == place
@@ -182,43 +198,44 @@
     wts[1] = mm_nt(eye, pw_lo).astype(BF16)
 
     loads[0].wait()
-    row0 = lax.rem(me, 8) * 16
-    sel16 = (iota((16, 128), 1) == iota((16, 128), 0) + row0).astype(F32)
-    start = mm_nt(sel16, init_v[...], HI)
-    pltpu.make_async_remote_copy(
-        src_ref=recv1.at[pl.ds(0, NS - 1)], dst_ref=recv1.at[pl.ds(0, NS - 1)], send_sem=s1, recv_sem=r1,
-        device_id=(me, up_y), device_id_type=MESH,
-    ).wait_recv()
-
-    def step(p, state):
-        res[p] = state.astype(BF16)
-        piece = recv1[p].astype(F32)
-        decay = piece[16:17, :] + piece[17:18, :] + piece[18:19, :]
-        return decay * state + piece[0:16, :]
-
-    lax.fori_loop(0, NS, step, start)
-
-    def send2(i, carry):
-        q = shifted(me, i, 1)
-        pltpu.make_async_remote_copy(
-            src_ref=res.at[q], dst_ref=recv2.at[me], send_sem=s2, recv_sem=r2,
-            device_id=(q, y), device_id_type=MESH,
-        ).start()
-        return carry
-
-    lax.fori_loop(1, NS, send2, 0)
-    recv2[pl.ds(me, 1)] = res[pl.ds(me, 1)]
-    pltpu.make_async_remote_copy(
-        src_ref=recv2.at[pl.ds(0, NS - 1)], dst_ref=recv2.at[pl.ds(0, NS - 1)], send_sem=s2, recv_sem=r2,
-        device_id=(me, up_y), device_id_type=MESH,
-    ).wait_recv()
+    sel16 = (iota((16, 128), 1) == iota((16, 128), 0) + plane * 16).astype(F32)
+    state = mm_nt(sel16, init_v[...], HI)
+    exchanged(recv1, xsem_s.at[0], xsem_r.at[0]).wait_recv()
+    total = jnp.zeros((128, 128), F32)
+    decay = jnp.ones((1, 128), F32)
+    for j in range(NP):
+        inner[j] = total
+        through[j : j + 1, :] = decay
+        step = recv1[j, 128:144, :].astype(F32)
+        step = step[0:1, :] + step[1:2, :] + step[2:3, :]
+        total = step * total + recv1[j, 0:128, :].astype(F32)
+        decay = step * decay
+    r16 = iota((16, 128), 0)
+    tail = jnp.zeros((16, 128), F32)
+    for n, part in enumerate(split3(decay)):
+        tail = jnp.where(r16 == n, part.astype(F32), tail)
+    for j in range(NZ):
+        msg2[j, 0:16, :] = total[j * 16 : (j + 1) * 16, :].astype(BF16)
+        msg2[j, 16:32, :] = tail.astype(BF16)
+    exchange(msg2, recv2, xsem_s.at[1], xsem_r.at[1], True)
+    exchanged(recv2, xsem_s.at[1], xsem_r.at[1]).wait_recv()
+    for j in range(NZ):
+        msg3[j] = state.astype(BF16)
+        piece = recv2[j].astype(F32)
+        state = (piece[16:17, :] + piece[17:18, :] + piece[18:19, :]) * state + piece[0:16, :]
+    exchange(msg3, recv3, xsem_s.at[2], xsem_r.at[2], True)
+    exchanged(recv3, xsem_s.at[2], xsem_r.at[2]).wait_recv()
+    entry = recv3[...].astype(F32).reshape(128, 128)
+    for j in range(NP):
+        msg4[j] = (through[j : j + 1, :] * entry + inner[j]).astype(BF16)
+    exchange(msg4, recv4, xsem_s.at[3], xsem_r.at[3], False)
+    exchanged(recv4, xsem_s.at[3], xsem_r.at[3]).wait_recv()
 
     same_head = (iota((128, 128), 0) // 64 == iota((128, 128), 1) // 64).astype(BF16)
     c_bf = c_ref[...]
     for l in range(8):
         lanes = slice(l * 128, (l + 1) * 128)
-        entering = recv2[l * 8 : (l + 1) * 8].reshape(128, 128)
-        v = ybuf[:, lanes] + mm(c_bf, entering) * expcum[:, lanes]
+        v = ybuf[:, lanes] + mm(c_bf, recv4[l]) * expcum[:, lanes]
         v = v * szbuf[:, lanes]
         mean_sq = mm((v * v).astype(BF16), same_head) * (1.0 / 64.0)
         normed[:, lanes] = (v * lax.rsqrt(mean_sq + 1e-05) * ngain_ref[:, lanes]).astype(BF16)
@@ -265,40 +282,49 @@
     hid[...] = hidden
     disp[...] = mm(pick, hidden).astype(BF16).reshape(NS, SLOTS, SLICE)
 
-    for g in range(GROUPS):
-        def send_d(i, carry):
+    def spread(k, sent, landed, send_sem, recv_sem, sign):
+        def one(j, carry):
+            i = k * NP + j
             pltpu.make_async_remote_copy(
-                src_ref=disp.at[i], dst_ref=xs.at[0, i], send_sem=sd, recv_sem=rd.at[g],
-                device_id=(shifted(me, i, 1), y), device_id_type=MESH,
+                src_ref=sent.at[i], dst_ref=landed.at[i], send_sem=send_sem, recv_sem=recv_sem,
+                device_id=(shifted(me, DZ[k] * NP + j, sign), y), device_id_type=MESH,
             ).start()
             return carry
 
-        lax.fori_loop(max(1, g * GS), (g + 1) * GS, send_d, 0)
-    xs[0, 0] = disp[0]
+        lax.fori_loop(0 if DZ[k] else 1, NP, one, 0)
+
+    def gathered(k, landed, send_sem, recv_sem):
+        first = 0 if DZ[k] else 1
+        part = landed.at[pl.ds(k * NP + first, NP - first)]
+        return pltpu.make_async_remote_copy(
+            src_ref=part, dst_ref=part, send_sem=send_sem, recv_sem=recv_sem,
+            device_id=(me, up_y), device_id_type=MESH,
+        )
+
+    own_x = xs.at[0]
+    for k in range(NZ):
+        spread(k, disp, own_x, sd, rd.at[k], 1)
+    xs[0, OWN] = disp[OWN]
     for load in loads[3:]:
         load.wait()
 
     def ag_copy(g, k):
         src, dst, first, count, peer = (
-            (0, 1, 0, GS, up_y),
-            (0, 3, 0, GS, dn_y),
-            (1, 2, 0, GS // 2, up_y),
-            (3, 2, GS // 2, GS // 2, dn_y),
+            (0, 1, 0, NP, up_y),
+            (0, 3, 0, NP, dn_y),
+            (1, 2, 0, NP // 2, up_y),
+            (3, 2, NP // 2, NP // 2, dn_y),
         )[k]
-        part = pl.ds(g * GS + first, count)
+        part = pl.ds(g * NP + first, count)
         return pltpu.make_async_remote_copy(
             src_ref=xs.at[src, part], dst_ref=xs.at[dst, part],
             send_sem=ag_s.at[g, k], recv_sem=ag_r.at[g, k], device_id=(me, peer), device_id_type=MESH,
         )
 
-    def arrive(g):
-        count = GS - 1 if g == 0 else GS
-        part = xs.at[0, pl.ds((g + 1) * GS - count, count)]
-        pltpu.make_async_remote_copy(
-            src_ref=part, dst_ref=part, send_sem=sd, recv_sem=rd.at[g], device_id=(me, up_y), device_id_type=MESH,
-        ).wait_recv()
-        ag_copy(g, 0).start()
-        ag_copy(g, 1).start()
+    def arrive(k):
+        gathered(k, own_x, sd, rd.at[k]).wait_recv()
+        ag_copy(k, 0).start()
+        ag_copy(k, 1).start()
 
     def forward(g):
         ag_copy(g, 0).wait_recv()
@@ -307,8 +333,9 @@
         ag_copy(g, 3).start()
 
     def expert(g):
-        ag_copy(g, 2).wait_recv()
-        ag_copy(g, 3).wait_recv()
+        for k in (2 * g, 2 * g + 1):
+            ag_copy(k, 2).wait_recv()
+            ag_copy(k, 3).wait_recv()
         accg[...] = jnp.zeros_like(accg)
         accu[...] = jnp.zeros_like(accu)
 
@@ -330,40 +357,57 @@
     def give_back(g):
         rets[g * GS : (g + 1) * GS] = rs_end(g).astype(BF16).reshape(GS, SLOTS, SLICE)
 
-        def send_r(i, carry):
-            pltpu.make_async_remote_copy(
-                src_ref=rets.at[i], dst_ref=retr.at[i], send_sem=sr, recv_sem=rr.at[g],
-                device_id=(shifted(me, i, -1), y), device_id_type=MESH,
-            ).start()
-            return carry
-
-        lax.fori_loop(max(1, g * GS), (g + 1) * GS, send_r, 0)
-
-    stages = (arrive, forward, expert, rs_middle, give_back)
-    for k in range(GROUPS + len(stages) - 1):
-        for n, stage in enumerate(stages):
-            if 0 <= k - n < GROUPS:
-                stage(k - n)
-
-    retr[0] = rets[0]
+        for k in (2 * g, 2 * g + 1):
+            spread(k, rets, retr, sr, rr.at[k], -1)
+
+    arrive(0)
+    arrive(1)
+    forward(0)
+    arrive(2)
+    forward(1)
+    arrive(3)
+    expert(0)
+    forward(2)
+    arrive(4)
+    forward(3)
+    arrive(5)
+    expert(1)
+    rs_middle(0)
+    forward(4)
+    arrive(6)
+    forward(5)
+    arrive(7)
+    expert(2)
+    rs_middle(1)
+    give_back(0)
+    forward(6)
+    forward(7)
+    expert(3)
+    rs_middle(2)
+    give_back(1)
+    rs_middle(3)
+    give_back(2)
+    give_back(3)
+
+    retr[OWN] = rets[OWN]
     total = hid[...].astype(F32)
     for g in range(GROUPS):
-        count = GS - 1 if g == 0 else GS
-        part = retr.at[pl.ds((g + 1) * GS - count, count)]
-        pltpu.make_async_remote_copy(
-            src_ref=part, dst_ref=part, send_sem=sr, recv_sem=rr.at[g], device_id=(me, up_y), device_id_type=MESH,
-        ).wait_recv()
+        for k in (2 * g, 2 * g + 1):
+            gathered(k, retr, sr, rr.at[k]).wait_recv()
         back = retr[g * GS : (g + 1) * GS].reshape(TOK, SLICE)
         lanes = slice(g * TOK, (g + 1) * TOK)
         total = total + mm(wts[0, :, lanes], back) + mm(wts[1, :, lanes], back)
     out_ref[...] = total.astype(BF16)
 
-    for buf, sem in ((msg1, s1), (res, s2), (disp, sd), (rets, sr)):
+    for n, buf in enumerate((msg1, msg2, msg3, msg4)):
+        exchanged(buf, xsem_s.at[n], xsem_r.at[n]).wait_send()
+    for buf, sem in ((disp, sd), (rets, sr)):
         part = buf.at[pl.ds(0, NS - 1)]
         pltpu.make_async_remote_copy(
-            src_ref=part, dst_ref=part, send_sem=sem, recv_sem=r1, device_id=(me, up_y), device_id_type=MESH,
+            src_ref=part, dst_ref=part, send_sem=sem, recv_sem=rd.at[0],
+            device_id=(me, up_y), device_id_type=MESH,
         ).wait_send()
-    for g in range(GROUPS):
+    for g in range(NZ):
         for k in range(4):
             ag_copy(g, k).wait_send()
     for n in range(GROUPS + 1):
@@ -380,10 +424,16 @@
     dma = pltpu.SemaphoreType.DMA
     n = GROUPS + 1
     scratch = [
-        pltpu.VMEM((NS, 24, 128), BF16),
-        pltpu.VMEM((NS, 24, 128), BF16),
-        pltpu.VMEM((NS, 16, 128), BF16),
-        pltpu.VMEM((NS, 16, 128), BF16),
+        pltpu.VMEM((NP, 144, 128), BF16),
+        pltpu.VMEM((NP, 144, 128), BF16),
+        pltpu.VMEM((NZ, 32, 128), BF16),
+        pltpu.VMEM((NZ, 32, 128), BF16),
+        pltpu.VMEM((NZ, 16, 128), BF16),
+        pltpu.VMEM((NZ, 16, 128), BF16),
+        pltpu.VMEM((NP, 128, 128), BF16),
+        pltpu.VMEM((NP, 128, 128), BF16),
+        pltpu.VMEM((NP, 128, 128), F32),
+        pltpu.VMEM((NP, 128), F32),
         pltpu.VMEM((TOK, INNER), F32),
         pltpu.VMEM((TOK, INNER), F32),
         pltpu.VMEM((TOK, INNER), F32),
@@ -408,10 +458,10 @@
         pltpu.VMEM((NS, SLOTS, SLICE), BF16),
         pltpu.VMEM((NS, SLOTS, SLICE), BF16),
         dma((6,)),
-        dma, dma, dma, dma,
-        dma, dma((GROUPS,)),
-        dma, dma((GROUPS,)),
-        dma((GROUPS, 4)), dma((GROUPS, 4)),
+        dma((4,)), dma((4,)),
+        dma, dma((NZ,)),
+        dma, dma((NZ,)),
+        dma((NZ, 4)), dma((NZ, 4)),
         dma((n, 4)), dma((n, 4)),
     ]
     return pl.pallas_call(
@@ -425,8 +475,8 @@
             collective_id=0, has_side_effects=True, vmem_limit_bytes=56 * 1024 * 1024
         ),
     )(
-        input_heads, z_gate, b_proj, c_proj, step_size, decay_log, skip_gain.reshape(1, HEADS),
-        norm_gain.reshape(1, INNER), moe_gain.reshape(1, WIDTH), routes, route_weights,
+        input_heads, z_gate, b_proj, c_proj, step_size.T, decay_log.T, skip_gain.reshape(1, HEADS),
+        norm_gain.reshape(1, INNER), moe_gain.reshape(1, WIDTH), routes.T, route_weights.T,
         tokens, init_state.reshape(INNER, 128), out_weight, w_gate[0], w_up[0], w_down[0],
     )
 

time: 114 us -> 104 us (0.912)
  local copies, waits for them, and re-layouts: 7.21 us -> 1.57 us
  Pallas kernels: 107 us -> 103 us
    unnamed x5 -> x1, local copies, waits for them, and re-layouts: 7.21 us -> 1.57 us
    pallas_call x1, Pallas kernels: 107 us -> 103 us  [body(): pl.pallas_call(kernel, out_shape=jax.ShapeDtypeStruct((TOK, SLICE), BF16)...]
where the time goes in v2:
time: 104 us
  Pallas kernels  103 us (99%)
  local copies, waits for them, and re-layouts  1.57 us (2%)
    pallas_call x1, Pallas kernels, body(): pl.pallas_call(kernel, out_shape=jax.ShapeDtypeStruct((TOK, SLICE), BF16)...  103 us

profile of v2, /device:TPU:1, one launch (start us, length us, event | category | flops | bytes accessed | tf_op | source)
XLA Modules:
  0.0 104.2 jit_solution(14169207306846696683)
XLA Ops:
  0.0 102.6 %mixer_moe.1 = bf16[128,512]{1,0:T(8,128)(2,1)} custom-call(bf16[128,1024]{1,0:T(8,128)(2,1)} %x_ref.1, bf16[128,1024]{1,0:T(8,128)(2,1)} %z_ref.1, bf16[128,128]{1,0:T(8,128)(2,1)} %b_ref.1, bf16[128,128]{1,0:T(8,128)(2,1)} %c_ref.1, f32[16,128]{1,0:T(8,128)} %bitcast.15, f32[16,128]{1,0:T(8,128)} %bitcast.16, f32[1,16]{1,0:T(1,128)} %bitcast.21, ...), custom_call_target="tpu_custom_call" | custom-call | tf_op jit(solution)/shard_map/mixer_moe/pallas_call | solution.py:467
  102.6 1.6 %copy.19 = bf16[128,512]{1,0:T(8,128)(2,1)} copy(bf16[128,512]{1,0:T(8,128)(2,1)} %mixer_moe.1) | data formatting | bytes 262144

commit v3 on v2

--- a/solution.py
+++ b/solution.py
@@ -21,19 +21,12 @@
 WIDTH = 2048
 SLICE = 512
 SLOTS = 8
-GROUPS = 4
+GROUPS = 8
 GS = NS // GROUPS
-DZ = (1, 7, 2, 6, 0, 4, 3, 5)
+GR = GS * SLOTS
+PAIRS = GROUPS // 2
+DZ = (0, 1, 7, 2, 6, 3, 5, 4)
 OWN = DZ.index(0) * NP
-
-
-def shifted(me, i, sign):
-    z, x, c = me // 8, lax.rem(me // 2, 4), lax.rem(me, 2)
-    dz, dx, dc = i // 8, lax.rem(i // 2, 4), lax.rem(i, 2)
-    z2 = lax.rem(z + NZ + sign * dz, NZ)
-    x2 = lax.rem(x + NX + sign * dx, NX)
-    c2 = lax.rem(c + NC + sign * dc, NC)
-    return z2 * 8 + x2 * 2 + c2
 
 
 def iota(shape, dim):
@@ -75,19 +68,22 @@
     dn_y = lax.rem(y + NY - 1, NY)
     far_y = lax.rem(y + 2, NY)
 
+    zme, xme, cme = me // NP, lax.rem(me, NP) // NC, lax.rem(me, NC)
+    planes = [lax.rem(zme + n, NZ) for n in range(NZ)]
+    z_terms = [z * NP for z in planes]
+    x_terms = [lax.rem(xme + n, NX) * NC for n in range(NX)]
+    c_terms = [cme, 1 - cme]
+    spots = [x_terms[n // NC] + c_terms[n % NC] for n in range(NP)]
+    spots_back = [x_terms[-(n // NC) % NX] + c_terms[n % NC] for n in range(NP)]
+
     barrier = pltpu.get_barrier_semaphore()
-
-    def greet(i, carry):
-        pl.semaphore_signal(barrier, inc=1, device_id=(shifted(me, i, 1), y), device_id_type=MESH)
-        return carry
-
-    lax.fori_loop(1, NP, greet, 0)
-    lax.fori_loop(1, NZ, lambda i, carry: greet(i * NP, carry), 0)
+    plane, spot = zme, spots[0]
+    for peer in [z_terms[0] + s for s in spots[1:]] + [z + spot for z in z_terms[1:]]:
+        pl.semaphore_signal(barrier, inc=1, device_id=(peer, y), device_id_type=MESH)
     for peer in (up_y, dn_y):
         pl.semaphore_signal(barrier, inc=1, device_id=(me, peer), device_id_type=MESH)
 
     own_col = pl.multiple_of(y * SLICE, SLICE)
-    plane, spot = me // NP, lax.rem(me, NP)
     tile_row = pl.multiple_of(spot * 128, 128)
     loads = [
         pltpu.make_async_copy(init_hbm.at[pl.ds(tile_row, 128), :], init_v, wsem.at[0]),
@@ -134,16 +130,13 @@
 
     def exchange(sent, landed, send_sem, recv_sem, across):
         mine = plane if across else spot
-
-        def one(i, carry):
-            q = shifted(me, i * NP if across else i, 1)
+        for n in range(1, NP):
+            other = planes[n] if across else spots[n]
+            peer = z_terms[n] + spot if across else z_terms[0] + spots[n]
             pltpu.make_async_remote_copy(
-                src_ref=sent.at[q // NP if across else lax.rem(q, NP)], dst_ref=landed.at[mine],
-                send_sem=send_sem, recv_sem=recv_sem, device_id=(q, y), device_id_type=MESH,
+                src_ref=sent.at[other], dst_ref=landed.at[mine],
+                send_sem=send_sem, recv_sem=recv_sem, device_id=(peer, y), device_id_type=MESH,
             ).start()
-            return carry
-
-        lax.fori_loop(1, NP, one, 0)
         landed[pl.ds(mine, 1)] = sent[pl.ds(mine, 1)]
 
     def exchanged(landed, send_sem, recv_sem):
@@ -175,7 +168,6 @@
 
     routes_t = routes_ref[...]
     rw_t = rw_ref[...]
-    zme, xme, cme = me // 8, lax.rem(me // 2, 4), lax.rem(me, 2)
     dz = ((routes_t >> 3) - zme + 8) & 7
     group = jnp.zeros_like(dz)
     for n, value in enumerate(DZ):
@@ -248,16 +240,22 @@
             device_id=(me, dn_y if side else up_y), device_id_type=MESH,
         )
 
-    half = TOK // 2
-
-    def rs_begin(n, lhs, w_v):
-        part = mm(lhs, w_v[:, pl.ds(pl.multiple_of(far_y * SLICE, SLICE), SLICE)]).astype(BF16)
-        far_s[n, 0] = part[:half]
-        far_s[n, 1] = part[half:]
-        rs_copy(n, 0).start()
-        rs_copy(n, 1).start()
+    half = GR // 2
+
+    def columns(w_v, where):
+        return w_v[:, pl.ds(pl.multiple_of(where * SLICE, SLICE), SLICE)]
+
+    def rs_begin(pair, lhs, w_v):
+        part = mm(lhs, columns(w_v, far_y)).astype(BF16)
+        for n in (0, 1):
+            far_s[2 * pair + n, 0] = part[n * GR : n * GR + half]
+            far_s[2 * pair + n, 1] = part[n * GR + half : (n + 1) * GR]
+            rs_copy(2 * pair + n, 0).start()
+            rs_copy(2 * pair + n, 1).start()
         for slot, where in ((0, up_y), (1, dn_y), (2, y)):
-            pbuf[n, slot] = mm(lhs, w_v[:, pl.ds(pl.multiple_of(where * SLICE, SLICE), SLICE)])
+            part = mm(lhs, columns(w_v, where))
+            pbuf[2 * pair, slot] = part[:GR]
+            pbuf[2 * pair + 1, slot] = part[GR:]
 
     def rs_middle(n):
         rs_copy(n, 0).wait_recv()
@@ -275,23 +273,23 @@
         return pbuf[n, 2] + near_r[n, 0].astype(F32) + near_r[n, 1].astype(F32)
 
     loads[2].wait()
-    rs_begin(GROUPS, normed[...], wout_v)
+    rs_begin(PAIRS, normed[...], wout_v)
     loads[1].wait()
     rs_middle(GROUPS)
-    hidden = (tok_v[...].astype(F32) + rs_end(GROUPS)).astype(BF16)
+    rs_middle(GROUPS + 1)
+    summed = jnp.concatenate([rs_end(GROUPS), rs_end(GROUPS + 1)], axis=0)
+    hidden = (tok_v[...].astype(F32) + summed).astype(BF16)
     hid[...] = hidden
     disp[...] = mm(pick, hidden).astype(BF16).reshape(NS, SLOTS, SLICE)
 
     def spread(k, sent, landed, send_sem, recv_sem, sign):
-        def one(j, carry):
+        for j in range(0 if DZ[k] else 1, NP):
             i = k * NP + j
+            dest = z_terms[sign * DZ[k] % NZ] + (spots if sign > 0 else spots_back)[j]
             pltpu.make_async_remote_copy(
                 src_ref=sent.at[i], dst_ref=landed.at[i], send_sem=send_sem, recv_sem=recv_sem,
-                device_id=(shifted(me, DZ[k] * NP + j, sign), y), device_id_type=MESH,
+                device_id=(dest, y), device_id_type=MESH,
             ).start()
-            return carry
-
-        lax.fori_loop(0 if DZ[k] else 1, NP, one, 0)
 
     def gathered(k, landed, send_sem, recv_sem):
         first = 0 if DZ[k] else 1
@@ -332,33 +330,32 @@
         ag_copy(g, 1).wait_recv()
         ag_copy(g, 3).start()
 
-    def expert(g):
-        for k in (2 * g, 2 * g + 1):
-            ag_copy(k, 2).wait_recv()
-            ag_copy(k, 3).wait_recv()
+    def expert(pair):
+        for g in (2 * pair, 2 * pair + 1):
+            ag_copy(g, 2).wait_recv()
+            ag_copy(g, 3).wait_recv()
         accg[...] = jnp.zeros_like(accg)
         accu[...] = jnp.zeros_like(accu)
 
         def piece(o, total):
             owner = lax.rem(y + NY - o, NY)
             at = pl.multiple_of(owner * SLICE, SLICE)
-            v = xs[o, pl.ds(g * GS, GS)].astype(F32).reshape(TOK, SLICE)
+            v = xs[o, pl.ds(2 * pair * GS, 2 * GS)].astype(F32).reshape(2 * GR, SLICE)
             vg = (v * mgain_ref[:, pl.ds(at, SLICE)]).astype(BF16)
             accg[...] += mm(vg, wg_v[pl.ds(at, SLICE), :])
             accu[...] += mm(vg, wu_v[pl.ds(at, SLICE), :])
             return total + jnp.sum(v * v, axis=1, keepdims=True)
 
-        total = lax.fori_loop(0, NY, piece, jnp.zeros((TOK, 1), F32))
+        total = lax.fori_loop(0, NY, piece, jnp.zeros((2 * GR, 1), F32))
         scale = lax.rsqrt(total * (1.0 / WIDTH) + 1e-05)
         gate = accg[...] * scale
         act = (0.5 * gate * (1.0 + jnp.tanh(0.5 * gate)) * (accu[...] * scale)).astype(BF16)
-        rs_begin(g, act, wd_v)
+        rs_begin(pair, act, wd_v)
 
     def give_back(g):
         rets[g * GS : (g + 1) * GS] = rs_end(g).astype(BF16).reshape(GS, SLOTS, SLICE)
 
-        for k in (2 * g, 2 * g + 1):
-            spread(k, rets, retr, sr, rr.at[k], -1)
+        spread(g, rets, retr, sr, rr.at[g], -1)
 
     arrive(0)
     arrive(1)
@@ -366,37 +363,45 @@
     arrive(2)
     forward(1)
     arrive(3)
-    expert(0)
     forward(2)
     arrive(4)
     forward(3)
     arrive(5)
-    expert(1)
-    rs_middle(0)
     forward(4)
+    expert(0)
     arrive(6)
     forward(5)
     arrive(7)
+    forward(6)
+    expert(1)
+    rs_middle(0)
+    rs_middle(1)
+    forward(7)
     expert(2)
-    rs_middle(1)
+    rs_middle(2)
+    rs_middle(3)
     give_back(0)
-    forward(6)
-    forward(7)
+    give_back(1)
     expert(3)
-    rs_middle(2)
-    give_back(1)
-    rs_middle(3)
+    rs_middle(4)
+    rs_middle(5)
     give_back(2)
     give_back(3)
+    rs_middle(6)
+    rs_middle(7)
+    give_back(4)
+    give_back(5)
+    give_back(6)
+    give_back(7)
 
     retr[OWN] = rets[OWN]
     total = hid[...].astype(F32)
     for g in range(GROUPS):
-        for k in (2 * g, 2 * g + 1):
-            gathered(k, retr, sr, rr.at[k]).wait_recv()
-        back = retr[g * GS : (g + 1) * GS].reshape(TOK, SLICE)
-        lanes = slice(g * TOK, (g + 1) * TOK)
-        total = total + mm(wts[0, :, lanes], back) + mm(wts[1, :, lanes], back)
+        gathered(g, retr, sr, rr.at[g]).wait_recv()
+        if g % 2:
+            back = retr[(g - 1) * GS : (g + 1) * GS].reshape(2 * GR, SLICE)
+            lanes = slice((g - 1) * GR, (g + 1) * GR)
+            total = total + mm(wts[0, :, lanes], back) + mm(wts[1, :, lanes], back)
     out_ref[...] = total.astype(BF16)
 
     for n, buf in enumerate((msg1, msg2, msg3, msg4)):
@@ -410,7 +415,7 @@
     for g in range(NZ):
         for k in range(4):
             ag_copy(g, k).wait_send()
-    for n in range(GROUPS + 1):
+    for n in range(GROUPS + 2):
         for k in range(4):
             rs_copy(n, k).wait_send()
 
@@ -422,7 +427,7 @@
     vmem = pl.BlockSpec(memory_space=pltpu.VMEM)
     hbm = pl.BlockSpec(memory_space=pl.ANY)
     dma = pltpu.SemaphoreType.DMA
-    n = GROUPS + 1
+    n = GROUPS + 2
     scratch = [
         pltpu.VMEM((NP, 144, 128), BF16),
         pltpu.VMEM((NP, 144, 128), BF16),
@@ -446,15 +451,15 @@
         pltpu.VMEM((SLICE, WIDTH), BF16),
         pltpu.VMEM((NS, SLOTS, SLICE), BF16),
         pltpu.VMEM((NY, NS, SLOTS, SLICE), BF16),
-        pltpu.VMEM((TOK, SLICE), F32),
-        pltpu.VMEM((TOK, SLICE), F32),
+        pltpu.VMEM((2 * GR, SLICE), F32),
+        pltpu.VMEM((2 * GR, SLICE), F32),
         pltpu.VMEM((TOK, SLICE), BF16),
         pltpu.VMEM((2, TOK, NS * SLOTS), BF16),
-        pltpu.VMEM((n, 2, TOK // 2, SLICE), BF16),
-        pltpu.VMEM((n, 2, TOK // 2, SLICE), BF16),
-        pltpu.VMEM((n, 2, TOK, SLICE), BF16),
-        pltpu.VMEM((n, 2, TOK, SLICE), BF16),
-        pltpu.VMEM((n, 3, TOK, SLICE), F32),
+        pltpu.VMEM((n, 2, GR // 2, SLICE), BF16),
+        pltpu.VMEM((n, 2, GR // 2, SLICE), BF16),
+        pltpu.VMEM((n, 2, GR, SLICE), BF16),
+        pltpu.VMEM((n, 2, GR, SLICE), BF16),
+        pltpu.VMEM((n, 3, GR, SLICE), F32),
         pltpu.VMEM((NS, SLOTS, SLICE), BF16),
         pltpu.VMEM((NS, SLOTS, SLICE), BF16),
         dma((6,)),

time: 104 us -> 95.7 us (0.920)
  Pallas kernels: 103 us -> 94 us
    pallas_call x1, Pallas kernels: 103 us -> 94 us  [body(): pl.pallas_call(kernel, out_shape=jax.ShapeDtypeStruct((TOK, SLICE), BF16)...]
where the time goes in v3:
time: 95.7 us; the launch traced here: 95.6 us
  Pallas kernels  94 us (98%)
  local copies, waits for them, and re-layouts  1.57 us (2%)
    pallas_call x1, Pallas kernels, body(): pl.pallas_call(kernel, out_shape=jax.ShapeDtypeStruct((TOK, SLICE), BF16)...  94 us

profile of v3, /device:TPU:1, one launch (start us, length us, event | category | flops | bytes accessed | tf_op | source)
XLA Modules:
  0.0 95.6 jit_solution(9444796480470008021)
XLA Ops:
  0.0 94.0 %mixer_moe.1 = bf16[128,512]{1,0:T(8,128)(2,1)} custom-call(bf16[128,1024]{1,0:T(8,128)(2,1)} %x_ref.1, bf16[128,1024]{1,0:T(8,128)(2,1)} %z_ref.1, bf16[128,128]{1,0:T(8,128)(2,1)} %b_ref.1, bf16[128,128]{1,0:T(8,128)(2,1)} %c_ref.1, f32[16,128]{1,0:T(8,128)} %bitcast.15, f32[16,128]{1,0:T(8,128)} %bitcast.16, f32[1,16]{1,0:T(1,128)} %bitcast.21, ...), custom_call_target="tpu_custom_call" | custom-call | tf_op jit(solution)/shard_map/mixer_moe/pallas_call | solution.py:472
  94.0 1.6 %copy.19 = bf16[128,512]{1,0:T(8,128)(2,1)} copy(bf16[128,512]{1,0:T(8,128)(2,1)} %mixer_moe.1) | data formatting | bytes 262144

commit v4 on v3

--- a/solution.py
+++ b/solution.py
@@ -27,6 +27,8 @@
 PAIRS = GROUPS // 2
 DZ = (0, 1, 7, 2, 6, 3, 5, 4)
 OWN = DZ.index(0) * NP
+FAR_Z = (4, 3, 5, 2, 6, 1, 7)
+FAR_SPOT = (4, 5, 2, 3, 6, 7, 1, 0)
 
 
 def iota(shape, dim):
@@ -78,7 +80,7 @@
 
     barrier = pltpu.get_barrier_semaphore()
     plane, spot = zme, spots[0]
-    for peer in [z_terms[0] + s for s in spots[1:]] + [z + spot for z in z_terms[1:]]:
+    for peer in [z_terms[n] + spot for n in FAR_Z] + [z_terms[0] + spots[n] for n in FAR_SPOT if n]:
         pl.semaphore_signal(barrier, inc=1, device_id=(peer, y), device_id_type=MESH)
     for peer in (up_y, dn_y):
         pl.semaphore_signal(barrier, inc=1, device_id=(me, peer), device_id_type=MESH)
@@ -130,7 +132,9 @@
 
     def exchange(sent, landed, send_sem, recv_sem, across):
         mine = plane if across else spot
-        for n in range(1, NP):
+        for n in FAR_Z if across else FAR_SPOT:
+            if n == 0:
+                continue
             other = planes[n] if across else spots[n]
             peer = z_terms[n] + spot if across else z_terms[0] + spots[n]
             pltpu.make_async_remote_copy(
@@ -283,7 +287,9 @@
     disp[...] = mm(pick, hidden).astype(BF16).reshape(NS, SLOTS, SLICE)
 
     def spread(k, sent, landed, send_sem, recv_sem, sign):
-        for j in range(0 if DZ[k] else 1, NP):
+        for j in FAR_SPOT:
+            if j == 0 and DZ[k] == 0:
+                continue
             i = k * NP + j
             dest = z_terms[sign * DZ[k] % NZ] + (spots if sign > 0 else spots_back)[j]
             pltpu.make_async_remote_copy(
@@ -300,7 +306,7 @@
         )
 
     own_x = xs.at[0]
-    for k in range(NZ):
+    for k in range(4):
         spread(k, disp, own_x, sd, rd.at[k], 1)
     xs[0, OWN] = disp[OWN]
     for load in loads[3:]:
@@ -323,6 +329,8 @@
         gathered(k, own_x, sd, rd.at[k]).wait_recv()
         ag_copy(k, 0).start()
         ag_copy(k, 1).start()
+        if k + 4 < NZ:
+            spread(k + 4, disp, own_x, sd, rd.at[k + 4], 1)
 
     def forward(g):
         ag_copy(g, 0).wait_recv()

time: 95.7 us -> 93.3 us (0.975)
  Pallas kernels: 94 us -> 91.7 us
    pallas_call x1, Pallas kernels: 94 us -> 91.7 us  [body(): pl.pallas_call(kernel, out_shape=jax.ShapeDtypeStruct((TOK, SLICE), BF16)...]
where the time goes in v4:
time: 93.3 us; the launch traced here: 93.2 us
  Pallas kernels  91.7 us (98%)
  local copies, waits for them, and re-layouts  1.57 us (2%)
    pallas_call x1, Pallas kernels, body(): pl.pallas_call(kernel, out_shape=jax.ShapeDtypeStruct((TOK, SLICE), BF16)...  91.7 us

profile of v4, /device:TPU:1, one launch (start us, length us, event | category | flops | bytes accessed | tf_op | source)
XLA Modules:
  0.0 93.2 jit_solution(1022201860134451179)
XLA Ops:
  0.0 91.7 %mixer_moe.1 = bf16[128,512]{1,0:T(8,128)(2,1)} custom-call(bf16[128,1024]{1,0:T(8,128)(2,1)} %x_ref.1, bf16[128,1024]{1,0:T(8,128)(2,1)} %z_ref.1, bf16[128,128]{1,0:T(8,128)(2,1)} %b_ref.1, bf16[128,128]{1,0:T(8,128)(2,1)} %c_ref.1, f32[16,128]{1,0:T(8,128)} %bitcast.15, f32[16,128]{1,0:T(8,128)} %bitcast.16, f32[1,16]{1,0:T(1,128)} %bitcast.21, ...), custom_call_target="tpu_custom_call" | custom-call | tf_op jit(solution)/shard_map/mixer_moe/pallas_call | solution.py:480
  91.7 1.6 %copy.19 = bf16[128,512]{1,0:T(8,128)(2,1)} copy(bf16[128,512]{1,0:T(8,128)(2,1)} %mixer_moe.1) | data formatting | bytes 262144

commit v5 on v4

--- a/solution.py
+++ b/solution.py
@@ -25,7 +25,7 @@
 GS = NS // GROUPS
 GR = GS * SLOTS
 PAIRS = GROUPS // 2
-DZ = (0, 1, 7, 2, 6, 3, 5, 4)
+DZ = (0, 1, 7, 3, 5, 4, 2, 6)
 OWN = DZ.index(0) * NP
 FAR_Z = (4, 3, 5, 2, 6, 1, 7)
 FAR_SPOT = (4, 5, 2, 3, 6, 7, 1, 0)

time: 93.3 us -> 93.2 us (level)
  no operation moved by 1% of the time
where the time goes in v5:
time: 93.2 us; the launch traced here: 93.1 us
  Pallas kernels  91.5 us (98%)
  local copies, waits for them, and re-layouts  1.57 us (2%)
    pallas_call x1, Pallas kernels, body(): pl.pallas_call(kernel, out_shape=jax.ShapeDtypeStruct((TOK, SLICE), BF16)...  91.5 us

profile of v5, /device:TPU:1, one launch (start us, length us, event | category | flops | bytes accessed | tf_op | source)
XLA Modules:
  0.0 93.1 jit_solution(18131731838902663323)
XLA Ops:
  0.0 91.5 %mixer_moe.1 = bf16[128,512]{1,0:T(8,128)(2,1)} custom-call(bf16[128,1024]{1,0:T(8,128)(2,1)} %x_ref.1, bf16[128,1024]{1,0:T(8,128)(2,1)} %z_ref.1, bf16[128,128]{1,0:T(8,128)(2,1)} %b_ref.1, bf16[128,128]{1,0:T(8,128)(2,1)} %c_ref.1, f32[16,128]{1,0:T(8,128)} %bitcast.15, f32[16,128]{1,0:T(8,128)} %bitcast.16, f32[1,16]{1,0:T(1,128)} %bitcast.21, ...), custom_call_target="tpu_custom_call" | custom-call | tf_op jit(solution)/shard_map/mixer_moe/pallas_call | solution.py:480
  91.5 1.6 %copy.19 = bf16[128,512]{1,0:T(8,128)(2,1)} copy(bf16[128,512]{1,0:T(8,128)(2,1)} %mixer_moe.1) | data formatting | bytes 262144
